TPU v7x, 32 devices: a whole 2x2x4 slice. The times are simulated.
32 devices in a mesh: rep: 16 (over z, y, core), grp: 2 (over x).
Axes of the slice: x: 2, y: 2, z: 4, core: 2. Of those that a mesh axis runs over, the one named last changes fastest.
Arguments:
- tokens: bfloat16 [16, 256, 1024], P('rep', 'grp'), may hold values from -24 to 24
- cotangent: bfloat16 [16, 256, 1024], P('rep', 'grp'), may hold values from -6 to 6
- block_order: int32 [16, 4], P('rep'), may hold values from 0 to 3, each once within a row
- ln1_gain: float32 [1024], replicated, may hold values from 0.5 to 1.5
- ln1_bias: float32 [1024], replicated, may hold values from -1.5 to 1.5
- ln2_gain: float32 [1024], replicated, may hold values from 0.5 to 1.5
- ln2_bias: float32 [1024], replicated, may hold values from -1.5 to 1.5
- w_qkv: bfloat16 [1024, 3072], P('grp'), may hold values from -4 to 4
- qv_bias: float32 [2, 1024], replicated, may hold values from -1.5 to 1.5
- w_out: bfloat16 [1024, 1024], P('grp'), may hold values from -1.5 to 1.5
- w_fc1: bfloat16 [1024, 4096], P('grp'), may hold values from -0.1875 to 0.1875
- fc1_bias: float32 [4096], replicated, may hold values from -1.5 to 1.5
- w_fc2: bfloat16 [4096, 1024], P('grp'), may hold values from -0.09375 to 0.09375
- fc2_bias: float32 [1024], replicated, may hold values from -1.5 to 1.5
Outputs:
- output: bfloat16 [16, 256, 1024], P('rep', 'grp')
- input_grad: float32 [16, 256, 1024], P('rep', 'grp')
- ln1_gain_grad: float32 [1024], P('grp')
- ln1_bias_grad: float32 [1024], P('grp')
- ln2_gain_grad: float32 [1024], P('grp')
- ln2_bias_grad: float32 [1024], P('grp')
- qkv_grad: float32 [1024, 3072], P('grp')
- qv_bias_grad: float32 [2, 1024], P(None, 'grp')
- out_grad: float32 [1024, 1024], P('grp')
- fc1_grad: float32 [1024, 4096], P('grp')
- fc1_bias_grad: float32 [4096], P('grp')
- fc2_grad: float32 [4096, 1024], P('grp')
- fc2_bias_grad: float32 [1024], P('grp')
Inputs may be any that keep to these rules, and one draw needn't show every extreme that they name: `block_order`: each row lists every block number once.
All inputs are finite; a program needn't handle non-finite values.
Results may differ from a plain program's by a relative error of at most 0.0087.
Values may be sent and summed in bfloat16 or wider, within the bound.
A program may use at most 256 MiB of HBM per device.

v0:
```python
import jax
import jax.numpy as jnp
from jax import lax
from jax.sharding import PartitionSpec as P

D = 1024
HEADS = 16
HEAD = 64
ROT = 16


EPS = 1e-05
NEGATIVE = -1e30


def rotary_tables(positions):
    half = ROT // 2
    frequency = 10000.0 ** (-jnp.arange(half, dtype=jnp.float32) * (2.0 / ROT))
    angles = positions.astype(jnp.float32)[:, None] * frequency[None, :]
    return (jnp.cos(angles)[:, None, :], jnp.sin(angles)[:, None, :])


def rotate(values, cosine, sine):
    half = ROT // 2
    first_half = values[..., :half]
    second_half = values[..., half:ROT]
    return jnp.concatenate(
        [
            first_half * cosine - second_half * sine,
            second_half * cosine + first_half * sine,
            values[..., ROT:],
        ],
        -1,
    )


def unrotate(values, cosine, sine):
    half = ROT // 2
    first_half = values[..., :half]
    second_half = values[..., half:ROT]
    return jnp.concatenate(
        [
            first_half * cosine + second_half * sine,
            second_half * cosine - first_half * sine,
            values[..., ROT:],
        ],
        -1,
    )


def norm_forward(inputs, gain, shift):
    centre = inputs - jnp.mean(inputs, -1, keepdims=True)
    scale_inv = lax.rsqrt(jnp.mean(centre * centre, -1, keepdims=True) + EPS)
    normed = centre * scale_inv
    return (normed, scale_inv, (normed * gain + shift).astype(jnp.bfloat16))


def norm_backward(upstream, normed, scale_inv, gain):
    scaled = upstream * gain
    return scale_inv * (
        scaled
        - jnp.mean(scaled, -1, keepdims=True)
        - normed * jnp.mean(scaled * normed, -1, keepdims=True)
    )


def gelu_exact(hidden):
    return 0.5 * hidden * (1.0 + lax.erf(hidden * 0.7071067811865476))


def gelu_slope(hidden):
    return (
        0.5 * (1.0 + lax.erf(hidden * 0.7071067811865476))
        + hidden * jnp.exp(-0.5 * hidden * hidden) * 0.3989422804014327
    )


def contract_last(left, right):
    return lax.dot_general(
        left, right, (((1,), (1,)), ((), ())), preferred_element_type=jnp.float32
    )


def contract_first(left, right):
    return lax.dot_general(
        left, right, (((0,), (0,)), ((), ())), preferred_element_type=jnp.float32
    )


def body(
    tokens,
    cotangent,
    block_order,
    ln1_gain,
    ln1_bias,
    ln2_gain,
    ln2_bias,
    w_qkv,
    qv_bias,
    w_out,
    w_fc1,
    fc1_bias,
    w_fc2,
    fc2_bias,
):
    float_type = jnp.float32
    group_size = lax.axis_size("grp")
    member = lax.axis_index("grp")
    inputs_b = tokens[0]
    upstream = cotangent[0]
    tok_count = inputs_b.shape[0]
    seq_total = tok_count * group_size
    block_size = tok_count // 2
    score_scale = HEAD ** (-0.5)
    row_ids = jnp.arange(seq_total, dtype=jnp.int32)
    block_ids = jnp.arange(2 * group_size, dtype=jnp.int32)
    matches = (row_ids // block_size)[:, None] == block_ids[None, :]
    all_pos = (
        jnp.sum(jnp.where(matches, block_order[0][None, :], 0), 1) * block_size
        + row_ids % block_size
    )
    own_pos = lax.dynamic_slice_in_dim(all_pos, member * tok_count, tok_count)
    cosine, sine = rotary_tables(own_pos)
    inputs = inputs_b.astype(float_type)
    normed_one, rstd_one, scaled_one = norm_forward(inputs, ln1_gain, ln1_bias)
    normed_two, rstd_two, scaled_two = norm_forward(inputs, ln2_gain, ln2_bias)
    qkv_full, out_full, up_full, down_full = (
        lax.all_gather(w_qkv, "grp", axis=0, tiled=True),
        lax.all_gather(w_out, "grp", axis=0, tiled=True),
        lax.all_gather(w_fc1, "grp", axis=0, tiled=True),
        lax.all_gather(w_fc2, "grp", axis=0, tiled=True),
    )
    qkv = jnp.dot(scaled_one, qkv_full, preferred_element_type=float_type)
    hidden = jnp.dot(scaled_two, up_full, preferred_element_type=float_type)
    hidden = hidden + fc1_bias
    query = (qkv[:, :D] + qv_bias[0]).reshape(tok_count, HEADS, HEAD)
    keys = qkv[:, D : 2 * D].reshape(tok_count, HEADS, HEAD)
    value_b = (qkv[:, 2 * D :] + qv_bias[1]).astype(jnp.bfloat16)
    query_b = rotate(query, cosine, sine).astype(jnp.bfloat16)
    keys_b = rotate(keys, cosine, sine).astype(jnp.bfloat16).reshape(tok_count, D)
    keys_all, values_all = (
        lax.all_gather(keys_b, "grp", axis=0, tiled=True),
        lax.all_gather(value_b, "grp", axis=0, tiled=True),
    )
    keys_all = keys_all.reshape(seq_total, HEADS, HEAD)
    values_all = values_all.reshape(seq_total, HEADS, HEAD)
    allowed = own_pos[None, :, None] >= all_pos[None, None, :]
    raw = (
        jnp.einsum("qhd,khd->hqk", query_b, keys_all, preferred_element_type=float_type)
        * score_scale
    )
    scores = jnp.where(allowed, raw, NEGATIVE)
    highest = jnp.max(scores, -1, keepdims=True)
    log_total = highest + jnp.log(jnp.sum(jnp.exp(scores - highest), -1, keepdims=True))
    prob_b = jnp.exp(scores - log_total).astype(jnp.bfloat16)
    mixed = (
        jnp.einsum("hqk,khd->qhd", prob_b, values_all, preferred_element_type=float_type)
        .astype(jnp.bfloat16)
        .reshape(tok_count, D)
    )
    act_b = gelu_exact(hidden).astype(jnp.bfloat16)
    attn_branch = jnp.dot(mixed, out_full, preferred_element_type=float_type)
    mlp_branch = jnp.dot(act_b, down_full, preferred_element_type=float_type)
    result = (inputs + attn_branch + mlp_branch + fc2_bias).astype(jnp.bfloat16)
    upstream_f = upstream.astype(float_type)
    d_act = contract_last(upstream, down_full)
    d_mixed = contract_last(upstream, out_full)
    d_hidden = d_act * gelu_slope(hidden)
    d_hidden_b = d_hidden.astype(jnp.bfloat16)
    d_mixed_b = d_mixed.astype(jnp.bfloat16).reshape(tok_count, HEADS, HEAD)
    prob_f = jnp.exp(scores - log_total)
    d_prob = jnp.einsum("qhd,khd->hqk", d_mixed_b, values_all, preferred_element_type=float_type)
    delta = jnp.sum(prob_f * d_prob, -1, keepdims=True)
    d_score = (prob_f * (d_prob - delta) * score_scale).astype(jnp.bfloat16)
    d_query = jnp.einsum("hqk,khd->qhd", d_score, keys_all, preferred_element_type=float_type)
    d_query = unrotate(d_query, cosine, sine).reshape(tok_count, D)
    key_part = jnp.einsum("hqk,qhd->khd", d_score, query_b, preferred_element_type=float_type)
    value_part = jnp.einsum("hqk,qhd->khd", prob_b, d_mixed_b, preferred_element_type=float_type)
    key_value_sum = lax.psum_scatter(
        jnp.stack(
            [
                key_part.reshape(tok_count * lax.axis_size("grp"), D),
                value_part.reshape(tok_count * lax.axis_size("grp"), D),
            ],
            1,
        ),
        "grp",
        scatter_dimension=0,
        tiled=True,
    )
    d_keys = unrotate(key_value_sum[:, 0].reshape(tok_count, HEADS, HEAD), cosine, sine).reshape(
        tok_count, D
    )
    d_value = key_value_sum[:, 1]
    d_qkv = jnp.concatenate([d_query, d_keys, d_value], 1).astype(jnp.bfloat16)
    d_one = contract_last(d_qkv, qkv_full)
    d_two = contract_last(d_hidden_b, up_full)
    qkv_group, hidden_group, upstream_group = (
        lax.all_gather(d_qkv, "grp", axis=0, tiled=True),
        lax.all_gather(d_hidden_b, "grp", axis=0, tiled=True),
        lax.all_gather(upstream, "grp", axis=0, tiled=True),
    )
    one_cols, two_cols, mixed_cols, act_cols = (
        lax.all_to_all(scaled_one, "grp", split_axis=1, concat_axis=0, tiled=True),
        lax.all_to_all(scaled_two, "grp", split_axis=1, concat_axis=0, tiled=True),
        lax.all_to_all(mixed, "grp", split_axis=1, concat_axis=0, tiled=True),
        lax.all_to_all(act_b, "grp", split_axis=1, concat_axis=0, tiled=True),
    )
    input_rows_grad = jnp.concatenate(
        [contract_first(one_cols, qkv_group), contract_first(two_cols, hidden_group)], 1
    )
    proj_rows_grad = contract_first(mixed_cols, upstream_group)
    down_rows_grad = contract_first(act_cols, upstream_group)
    gain_one, shift_one, gain_two, shift_two, qv_part, up_shift, down_shift = (
        lax.psum_scatter(jnp.sum(d_one * normed_one, 0), "grp", scatter_dimension=0, tiled=True),
        lax.psum_scatter(jnp.sum(d_one, 0), "grp", scatter_dimension=0, tiled=True),
        lax.psum_scatter(jnp.sum(d_two * normed_two, 0), "grp", scatter_dimension=0, tiled=True),
        lax.psum_scatter(jnp.sum(d_two, 0), "grp", scatter_dimension=0, tiled=True),
        lax.psum_scatter(
            jnp.stack([jnp.sum(d_query, 0), jnp.sum(d_value, 0)]),
            "grp",
            scatter_dimension=1,
            tiled=True,
        ),
        lax.psum_scatter(jnp.sum(d_hidden, 0), "grp", scatter_dimension=0, tiled=True),
        lax.psum_scatter(jnp.sum(upstream_f, 0), "grp", scatter_dimension=0, tiled=True),
    )
    summed = lax.psum(
        (
            input_rows_grad,
            proj_rows_grad,
            down_rows_grad,
            gain_one,
            shift_one,
            gain_two,
            shift_two,
            qv_part,
            up_shift,
            down_shift,
        ),
        "rep",
    )
    grad_in = (
        upstream_f
        + norm_backward(d_one, normed_one, rstd_one, ln1_gain)
        + norm_backward(d_two, normed_two, rstd_two, ln2_gain)
    )
    input_rows_total = summed[0]
    return (
        result[None],
        grad_in[None],
        summed[3],
        summed[4],
        summed[5],
        summed[6],
        input_rows_total[:, : 3 * D],
        summed[7],
        summed[1],
        input_rows_total[:, 3 * D :],
        summed[8],
        summed[2],
        summed[9],
    )


def solution(mesh):
    placed = (
        P("rep", "grp", None),
        P("rep", "grp", None),
        P("rep", None),
        P(),
        P(),
        P(),
        P(),
        P("grp", None),
        P(),
        P("grp", None),
        P("grp", None),
        P(),
        P("grp", None),
        P(),
    )
    return jax.shard_map(
        body,
        mesh=mesh,
        in_specs=placed,
        out_specs=(
            P("rep", "grp", None),
            P("rep", "grp", None),
            P("grp"),
            P("grp"),
            P("grp"),
            P("grp"),
            P("grp", None),
            P(None, "grp"),
            P("grp", None),
            P("grp", None),
            P("grp"),
            P("grp", None),
            P("grp"),
        ),
        check_vma=False,
    )
```

profile of v0, /device:TPU:0, one launch (start us, length us, event | category | flops | bytes accessed | tf_op | source)
XLA Modules:
  0.0 943.4 jit_solution(15967782235575554713)
XLA Ops:
  7.2 0.7 all-gather.10.cloned.1.call-update
  8.0 0.7 all-gather.8.cloned.1.call-update
  8.7 0.7 all-gather.12.cloned.1.call-update
  11.0 34.4 %all-gather.10.cloned.1.call-done = bf16[1024,1024]{1,0:T(8,128)(2,1)} async-done(((bf16[512,1024]{1,0:T(8,128)(2,1)}), bf16[1024,1024]{1,0:T(8,128)(2,1)}) %all-gather.10.cloned.1.call-update) | async-done | bytes 2097168 | tf_op jit(solution)/shard_map/all_gather | solution.py:129
  45.4 2.4 convolution_convert_fusion
  48.0 79.3 %all-gather.8.cloned.1.call-done = bf16[1024,3072]{1,0:T(8,128)(2,1)} async-done(((bf16[512,3072]{1,0:T(8,128)(2,1)}), bf16[1024,3072]{1,0:T(8,128)(2,1)}) %all-gather.8.cloned.1.call-update) | async-done | bytes 6291472 | tf_op jit(solution)/shard_map/all_gather | solution.py:128
  127.4 3.9 fusion.43
  131.6 0.7 slice.135
  132.5 8.6 all_gather.28
  141.4 14.7 %all_gather.29 = bf16[256,1024]{0,1:T(8,128)(2,1)S(1)} all-gather(bf16[128,1024]{0,1:T(8,128)(2,1)S(1)} %bitcast.135), channel_id=1, replica_groups=mesh['rep'=16,'grp'=2] {'grp'}, dimensions={0}, use_global_device_ids=true | all-gather | bytes 786432 | tf_op jit(solution)/shard_map/all_gather | solution.py:142
  156.1 0.8 copy-done.20
  156.9 1.5 fusion.67
  158.4 0.6 exponential_reduce_fusion
  159.1 1.8 fusion.69
  160.9 14.5 %fusion.9 = f32[16,64,256]{2,1,0:T(8,128)} fusion(f32[16,128,256]{2,1,0:T(8,128)} %fusion.69, f32[16,128,256]{2,1,0:T(8,128)S(1)} %get-tuple-element.73, f32[16,128]{1,0:T(8,128)S(1)} %log_add_fusion, bf16[128,16,48]{0,2,1:T(8,128)(2,1)S(1)} %copy-done.21, bf16[128,16,8]{0,2,1:T(8,128)(2,1)S(1)} %get-tuple-element.55, ...), kind=kOutput, calls=%fused_computation.18 | convolution fusion | flops 71567616 | bytes 5513216 | tf_op jit(solution)/shard_map/hqk,qhd->khd/dot_general | solution.py:177
  175.4 0.8 fusion.39
  176.6 1.5 pad_maximum_fusion.1
  178.4 60.2 %all-gather.12.cloned.1.call-done = bf16[1024,4096]{1,0:T(8,128)(2,1)} async-done(((bf16[512,4096]{1,0:T(8,128)(2,1)}), bf16[1024,4096]{1,0:T(8,128)(2,1)}) %all-gather.12.cloned.1.call-update) | async-done | bytes 8388624 | tf_op jit(solution)/shard_map/all_gather | solution.py:130
  238.6 6.5 multiply_convert_fusion.1
  245.0 98.9 %all-gather.14.cloned.1.call-done = bf16[4096,1024]{1,0:T(8,128)(2,1)} async-done(((bf16[2048,1024]{1,0:T(8,128)(2,1)}), bf16[4096,1024]{1,0:T(8,128)(2,1)}) %all-gather.14.cloned.1.call-update) | async-done | bytes 8388624 | tf_op jit(solution)/shard_map/all_gather | solution.py:131
  343.9 8.7 fusion.65
  355.1 1.3 reshape.271
  356.4 14.5 %fusion.15 = f32[128,16,64]{0,2,1:T(8,128)} fusion(bf16[256,16,64]{0,2,1:T(8,128)(2,1)} %bitcast.144, f32[16,128,256]{2,1,0:T(8,128)} %fusion.69, f32[16,128,256]{2,1,0:T(8,128)S(1)} %get-tuple-element.73, f32[16,128]{1,0:T(8,128)S(1)} %log_add_fusion), kind=kOutput, calls=%fused_computation.21 | convolution fusion | flops 70781184 | bytes 5251072 | tf_op jit(solution)/shard_map/hqk,khd->qhd/dot_general | solution.py:175
  371.0 1.8 slice.98
  372.7 5.8 reduce-scatter.5.cloned.1.call-done
  378.5 2.1 slice_reduce_fusion
  380.6 0.9 multiply_add_fusion
  381.7 1.3 fusion.42
  383.0 0.7 copy-done.16
  383.6 0.9 pad_maximum_fusion.2
  384.6 2.3 convolution_convert_fusion.1
  386.9 1.8 copy.58
  388.7 3.4 all-to-all-start.2
  392.2 20.2 %all-gather = bf16[1,256,1024]{2,1,0:T(8,128)(2,1)S(1)} all-gather(bf16[1,128,1024]{2,1,0:T(8,128)(2,1)} %param.15), channel_id=2, replica_groups=mesh['rep'=16,'grp'=2] {'grp'}, dimensions={1}, use_global_device_ids=true | all-gather | bytes 786432 | tf_op jit(solution)/shard_map/all_gather | solution.py:201
  412.4 1.0 copy.71
  413.5 0.7 copy-done.19
  414.2 3.6 all-to-all-start.3
  417.8 1.9 add_convert_fusion.1
  419.7 2.7 fusion.33
  422.4 10.1 %all-to-all-done.3 = bf16[128,2,2048]{2,0,1:T(8,128)(2,1)S(1)} async-done(((bf16[128,2,2048]{2,0,1:T(8,128)(2,1)}), bf16[128,2,2048]{2,0,1:T(8,128)(2,1)S(1)}, u32[]{:S(2)}, u32[]{:S(2)}) %all-to-all-start.3) | async-done | bytes 1048608 | tf_op jit(solution)/shard_map/all_to_all | solution.py:207
  432.5 3.4 all-to-all-start.1
  436.0 4.7 fusion.31
  441.0 1.0 copy.60
  442.1 2.8 all-to-all-done.1
  444.9 3.4 all-to-all-start
  448.6 6.3 fusion.72
  454.9 2.1 all-to-all-done
  457.5 2.6 fusion.71
  460.1 1.3 copy-done
  461.3 5.7 pad_maximum_fusion
  467.0 0.6 copy-done.38
  469.6 4.8 fusion.68
  474.4 1.2 fusion.21
  475.7 6.8 fusion.70
  482.5 2.5 multiply_reduce_fusion.2
  485.0 1.2 convert_reduce_fusion
  486.2 7.1 all-reduce.8
  493.8 1.1 copy.61
  494.8 63.4 %all-reduce.6 = (f32[512]{0:T(512)}, f32[512]{0:T(512)}, f32[512]{0:T(512)}, f32[512]{0:T(512)}, f32[2,512]{1,0:T(2,128)}, /*index=5*/f32[2048]{0:T(1024)}, f32[512]{0:T(512)}) all-reduce(f32[512]{0:T(512)S(1)} %dynamic-slice.1, f32[512]{0:T(512)S(1)} %dynamic-slice.3, ...), channel_id=1, replica_groups=mesh['rep'=16,'grp'=2] {'rep'}, use_global_device_ids=true, to_apply=%region_13.14 | all-reduce | flops 5632 | bytes 45056 | tf_op jit(solution)/shard_map/psum | solution.py:228
  558.2 359.6 %all-reduce.11.cloned.1.call-done = (f32[512,7168]{1,0:T(8,128)}, f32[512,1024]{1,0:T(8,128)}, f32[2048,1024]{1,0:T(8,128)}) async-done(((f32[512,7168]{1,0:T(8,128)}, f32[512,1024]{1,0:T(8,128)}, f32[2048,1024]{1,0:T(8,128)}), (f32[512,7168]{1,0:T(8,128)}, f32[512,1024]{1,0:T(8,128)}, f32[2048,1024]{1,0:T(8,128)})) %all-reduce.11.cloned.1.call-update) | async-done | bytes 25165840 | tf_op jit(solution)/shard_map/psum | solution.py:228
  917.8 6.4 slice.104
  924.2 7.9 slice.105
  932.1 1.3 copy.75
  933.5 3.4 copy.76
  (143 shorter events, 8.1 us)
Async XLA Ops:
  7.2 38.2 %all-gather.10.cloned.1.call-start = ((), (), s32[]{:S(2)}) async-start(), calls=%async_computation.7 | async-start | bytes 3145728 | tf_op jit(solution)/shard_map/all_gather | solution.py:129
  7.9 119.4 %all-gather.8.cloned.1.call-start = ((), (), s32[]{:S(2)}) async-start(), calls=%async_computation.6 | async-start | bytes 9437184 | tf_op jit(solution)/shard_map/all_gather | solution.py:128
  8.7 229.9 %all-gather.12.cloned.1.call-start = ((), (), s32[]{:S(2)}) async-start(), calls=%async_computation.8 | async-start | bytes 12582912 | tf_op jit(solution)/shard_map/all_gather | solution.py:130
  9.4 0.7 copy-start.37
  9.4 1.0 copy-start.1
  9.4 1.4 copy-start.35
  9.4 36.0 %copy-start.7 = (bf16[1,128,1024]{2,1,0:T(8,128)(2,1)S(1)}, bf16[1,128,1024]{2,1,0:T(8,128)(2,1)}, u32[]{:S(2)}) copy-start(bf16[1,128,1024]{2,1,0:T(8,128)(2,1)} %param.15) | copy-start | bytes 786436
  9.4 334.5 %all-gather.14.cloned.1.call-start = ((), (), s32[]{:S(2)}) async-start(), calls=%async_computation.9 | async-start | bytes 12582912 | tf_op jit(solution)/shard_map/all_gather | solution.py:131
  10.0 117.3 %copy-start.22 = (f32[1024]{0:T(1024)S(1)}, f32[1024]{0:T(1024)}, u32[]{:S(2)}) copy-start(f32[1024]{0:T(1024)} %param.17) | copy-start | bytes 12292
  10.0 117.3 %copy-start.24 = (f32[1024]{0:T(1024)S(1)}, f32[1024]{0:T(1024)}, u32[]{:S(2)}) copy-start(f32[1024]{0:T(1024)} %param.18) | copy-start | bytes 12292
  10.0 368.5 %reduce-scatter.5.cloned.1.call-start = ((), (), s32[]{:S(2)}) async-start(), calls=%async_computation.10 | async-start | bytes 3145728 | tf_op jit(solution)/shard_map/reduce_scatter | solution.py:179
  10.5 228.0 %copy-start.28 = (f32[128]{0:T(128)}, f32[128]{0:T(128)S(1)}, u32[]{:S(2)}) copy-start(f32[128]{0:T(128)S(1)} %broadcast_multiply_fusion.4) | copy-start | bytes 1540
  10.7 227.8 %copy-start.30 = (f32[128]{0:T(128)}, f32[128]{0:T(128)S(1)}, u32[]{:S(2)}) copy-start(f32[128]{0:T(128)S(1)} %add_rsqrt_fusion) | copy-start | bytes 1540
  10.9 130.4 %copy-start.26 = (f32[128,8]{0,1:T(8,128)}, f32[128,8]{0,1:T(8,128)S(1)}, u32[]{:S(2)}) copy-start(f32[128,8]{0,1:T(8,128)S(1)} %get-tuple-element.68) | copy-start | bytes 12292
  10.9 130.4 %copy-start.27 = (f32[128,8]{0,1:T(8,128)}, f32[128,8]{0,1:T(8,128)S(1)}, u32[]{:S(2)}) copy-start(f32[128,8]{0,1:T(8,128)S(1)} %get-tuple-element.69) | copy-start | bytes 12292
  141.3 17.8 %copy-start.3 = (bf16[256,1024]{0,1:T(8,128)(2,1)}, bf16[256,1024]{0,1:T(8,128)(2,1)S(1)}, u32[]{:S(2)}) copy-start(bf16[256,1024]{0,1:T(8,128)(2,1)S(1)} %copy.53) | copy-start | bytes 1572868
  156.1 0.8 copy-start.20
  158.4 2.5 copy-start.21
  175.4 1.2 copy-start.18
  178.1 60.4 %copy-start.23 = (f32[1024]{0:T(1024)S(1)}, f32[1024]{0:T(1024)}, u32[]{:S(2)}) copy-start(f32[1024]{0:T(1024)} %param.19) | copy-start | bytes 12292
  178.1 60.4 %copy-start.25 = (f32[1024]{0:T(1024)S(1)}, f32[1024]{0:T(1024)}, u32[]{:S(2)}) copy-start(f32[1024]{0:T(1024)} %param.20) | copy-start | bytes 12292
  178.1 60.4 %copy-start.34 = (f32[4096]{0:T(1024)S(1)}, f32[4096]{0:T(1024)}, u32[]{:S(2)}) copy-start(f32[4096]{0:T(1024)} %param.25) | copy-start | bytes 49156
  178.1 270.5 %all-gather.18.cloned.1.call-start = ((), (), s32[]{:S(2)}) async-start(), calls=%async_computation.12 | async-start | bytes 3145728 | tf_op jit(solution)/shard_map/all_gather | solution.py:200
  352.7 104.8 %all-gather.16.cloned.1.call-start = ((), (), s32[]{:S(2)}) async-start(), calls=%async_computation.11 | async-start | bytes 2359296 | tf_op jit(solution)/shard_map/all_gather | solution.py:199
  378.5 3.0 copy-start.5
  381.7 1.3 copy-start.12
  381.7 1.3 copy-start.14
  382.9 0.7 copy-start.16
  388.7 24.7 %all-to-all-start.2 = ((bf16[128,2,512]{2,0,1:T(8,128)(2,1)}), bf16[128,2,512]{2,0,1:T(8,128)(2,1)S(1)}, u32[]{:S(2)}, u32[]{:S(2)}) async-start(bf16[128,2,512]{2,0,1:T(8,128)(2,1)} %copy.58), calls=%async_computation.3 | async-start | bytes 524288 | tf_op jit(solution)/shard_map/all_to_all | solution.py:206
  412.4 5.3 copy-start.10
  412.4 5.4 copy-start.29
  412.4 5.4 copy-start.31
  413.5 0.7 copy-start.19
  414.2 18.3 %all-to-all-start.3 = ((bf16[128,2,2048]{2,0,1:T(8,128)(2,1)}), bf16[128,2,2048]{2,0,1:T(8,128)(2,1)S(1)}, u32[]{:S(2)}, u32[]{:S(2)}) async-start(bf16[128,2,2048]{2,0,1:T(8,128)(2,1)} %bitcast.121), calls=%async_computation.4 | async-start | bytes 2097152 | tf_op jit(solution)/shard_map/all_to_all | solution.py:207
  432.5 12.4 %all-to-all-start.1 = ((bf16[128,2,512]{2,0,1:T(8,128)(2,1)}), bf16[128,2,512]{2,0,1:T(8,128)(2,1)S(1)}, u32[]{:S(2)}, u32[]{:S(2)}) async-start(bf16[128,2,512]{2,0,1:T(8,128)(2,1)} %get-tuple-element.59), calls=%async_computation.2 | async-start | bytes 524288 | tf_op jit(solution)/shard_map/all_to_all | solution.py:205
  435.9 57.8 %reduce-scatter.7.cloned.1.call-start = ((), (), s32[]{:S(2)}) async-start(), calls=%async_computation.13 | async-start | bytes 786432
  436.0 4.7 copy-start.6
  436.0 5.0 copy-start.32
  444.9 12.1 %all-to-all-start = ((bf16[128,2,512]{2,0,1:T(8,128)(2,1)}), bf16[128,2,512]{2,0,1:T(8,128)(2,1)S(1)}, u32[]{:S(2)}, u32[]{:S(2)}) async-start(bf16[128,2,512]{2,0,1:T(8,128)(2,1)} %get-tuple-element.58), calls=%async_computation.1 | async-start | bytes 524288 | tf_op jit(solution)/shard_map/all_to_all | solution.py:204
  448.3 469.5 %all-reduce.11.cloned.1.call-start = ((), (), s32[]{:S(2)}) async-start(), calls=%async_computation.14 | async-start | bytes 50331648 | tf_op jit(solution)/shard_map/psum | solution.py:228
  457.5 3.9 copy-start
  467.0 0.7 copy-start.38
  469.5 4.9 copy-start.2
  469.5 4.9 copy-start.9
  469.5 4.9 copy-start.36
  474.4 1.2 copy-start.4
  474.4 8.0 slice-start
  475.6 6.8 slice-start.1
  475.6 6.8 copy-start.13
  475.6 6.8 copy-start.15
  475.7 6.8 copy-start.17
  482.5 2.5 copy-start.8
  485.0 1.2 copy-start.33
  917.8 15.6 %slice-start.2 = ((s8[8388608]{0:T(1024)(128)(4,1)}), s8[4194304]{0:T(1024)(128)(4,1)S(1)}, s32[]{:S(2)}) async-start(s8[8388608]{0:T(1024)(128)(4,1)} %bitcast.116), calls=%async_computation.17 | async-start | bytes 8388608
  924.2 7.9 copy-start.11
  924.2 9.3 slice-start.3
Sparse Core Ops, SparseCore 0:
  9.5 35.8 all-gather.9
  47.0 80.3 all-gather.7
  128.9 109.5 all-gather.11
  239.9 103.9 all-gather.13
  346.6 31.8 reduce-scatter.4
  379.9 42.7 all-gather.17
  424.3 33.1 all-gather.15
  460.3 14.6 reduce-scatter.6
  480.3 437.4 all-reduce.10
where the time goes:
time: 944 us; the launch traced here: 943 us
  waiting for transfers between devices  656 us (69%)
  blocking collectives  114 us (12%)
  matrix products  88.5 us (9%)
  local copies, waits for them, and re-layouts  38 us (4%)
  other arithmetic  16 us (2%)
  between operations  15.8 us (2%)
  starting transfers between devices  14.7 us (2%)
    psum x1, waiting for transfers between devices, body(): lax.psum((input_rows_grad, proj_rows_grad, down_rows_grad, gain_one, shif...  360 us
    all_gather x1, waiting for transfers between devices, body(): lax.all_gather(w_fc2, 'grp', axis=0, tiled=True)  98.9 us
    all_gather x1, waiting for transfers between devices, body(): lax.all_gather(w_qkv, 'grp', axis=0, tiled=True)  79.3 us
    psum x1, blocking collectives, body(): lax.psum((input_rows_grad, proj_rows_grad, down_rows_grad, gain_one, shif...  63.4 us
    all_gather x1, waiting for transfers between devices, body(): lax.all_gather(w_fc1, 'grp', axis=0, tiled=True)  60.2 us
    all_gather x1, waiting for transfers between devices, body(): lax.all_gather(w_out, 'grp', axis=0, tiled=True)  34.4 us
    dot_general x4, matrix products, contract_last(): lax.dot_general(left, right, (((1,), (1,)), ((), ())), preferred_element_...  20.4 us
    all_gather x1, blocking collectives, body(): lax.all_gather(upstream, 'grp', axis=0, tiled=True)  20.2 us
  transfers between devices with their start and end apart: 13, of which 10 were waited for; matrix products, arithmetic and copies ran while one was open for 13% of the time, Pallas kernels for 0%

commit v1 on v0

v1 whole, which is shorter than its diff:
```python
import jax
import jax.numpy as jnp
from jax import lax
from jax.sharding import PartitionSpec as P

D = 1024
HEADS = 16
HEAD = 64
ROT = 16


EPS = 1e-05
NEGATIVE = -1e30


def rotary_tables(positions):
    half = ROT // 2
    frequency = 10000.0 ** (-jnp.arange(half, dtype=jnp.float32) * (2.0 / ROT))
    angles = positions.astype(jnp.float32)[:, None] * frequency[None, :]
    return (jnp.cos(angles)[:, None, :], jnp.sin(angles)[:, None, :])


def rotate(values, cosine, sine):
    half = ROT // 2
    first_half = values[..., :half]
    second_half = values[..., half:ROT]
    return jnp.concatenate(
        [
            first_half * cosine - second_half * sine,
            second_half * cosine + first_half * sine,
            values[..., ROT:],
        ],
        -1,
    )


def unrotate(values, cosine, sine):
    half = ROT // 2
    first_half = values[..., :half]
    second_half = values[..., half:ROT]
    return jnp.concatenate(
        [
            first_half * cosine + second_half * sine,
            second_half * cosine - first_half * sine,
            values[..., ROT:],
        ],
        -1,
    )


def gelu_exact(hidden):
    return 0.5 * hidden * (1.0 + lax.erf(hidden * 0.7071067811865476))


def gelu_slope(hidden):
    return (
        0.5 * (1.0 + lax.erf(hidden * 0.7071067811865476))
        + hidden * jnp.exp(-0.5 * hidden * hidden) * 0.3989422804014327
    )


def contract_last(left, right):
    return lax.dot_general(
        left, right, (((1,), (1,)), ((), ())), preferred_element_type=jnp.float32
    )


def contract_first(left, right):
    return lax.dot_general(
        left, right, (((0,), (0,)), ((), ())), preferred_element_type=jnp.float32
    )


def shift(value, distance):
    size = lax.axis_size("grp")
    return lax.ppermute(value, "grp", [(i, (i + distance) % size) for i in range(size)])


def gather_along(value, axis):
    size = lax.axis_size("grp")
    member = lax.axis_index("grp")
    width = value.shape[axis]
    shape = list(value.shape)
    shape[axis] = width * size
    whole = jnp.zeros(shape, value.dtype)
    for step in range(size):
        block = value if step == 0 else shift(value, step)
        owner = (member - step) % size
        whole = lax.dynamic_update_slice_in_dim(whole, block, owner * width, axis)
    return whole


def scatter_sum(part_for):
    size = lax.axis_size("grp")
    member = lax.axis_index("grp")
    arrived = []
    for step in range(1, size):
        term = part_for((member + step) % size)
        arrived.append(shift(term.astype(jnp.bfloat16), step))
    total = part_for(member)
    for term in arrived:
        total = total + term.astype(jnp.float32)
    return total


def columns_of(value, owner, width):
    return lax.dynamic_slice_in_dim(value, owner * width, width, value.ndim - 1)


def rows_of(value, owner, width):
    return lax.dynamic_slice_in_dim(value, owner * width, width, 0)


def rep_sum(values):
    return lax.psum([value.astype(jnp.bfloat16) for value in values], "rep")


def body(
    tokens,
    cotangent,
    block_order,
    ln1_gain,
    ln1_bias,
    ln2_gain,
    ln2_bias,
    w_qkv,
    qv_bias,
    w_out,
    w_fc1,
    fc1_bias,
    w_fc2,
    fc2_bias,
):
    float_type = jnp.float32
    half_type = jnp.bfloat16
    group_size = lax.axis_size("grp")
    member = lax.axis_index("grp")
    tok_count = tokens.shape[1]
    seq_total = tok_count * group_size
    block_size = tok_count // 2
    own_width = D // group_size
    own_heads = HEADS // group_size
    own_hidden = w_fc2.shape[0]
    score_scale = HEAD ** (-0.5)

    pair = gather_along(jnp.concatenate([tokens[0], cotangent[0]], 1), 0)
    inputs_b = pair[:, :D]
    upstream = pair[:, D:]
    row_ids = jnp.arange(seq_total, dtype=jnp.int32)
    block_ids = jnp.arange(2 * group_size, dtype=jnp.int32)
    matches = (row_ids // block_size)[:, None] == block_ids[None, :]
    all_pos = (
        jnp.sum(jnp.where(matches, block_order[0][None, :], 0), 1) * block_size
        + row_ids % block_size
    )
    cosine, sine = rotary_tables(all_pos)

    inputs = inputs_b.astype(float_type)
    centre = inputs - jnp.mean(inputs, -1, keepdims=True)
    rstd = lax.rsqrt(jnp.mean(centre * centre, -1, keepdims=True) + EPS)
    normed_cols = columns_of(inputs, member, own_width)
    normed_cols = (normed_cols - jnp.mean(inputs, -1, keepdims=True)) * rstd
    gain_one = columns_of(ln1_gain, member, own_width)
    gain_two = columns_of(ln2_gain, member, own_width)
    one_cols = (normed_cols * gain_one + columns_of(ln1_bias, member, own_width)).astype(half_type)
    two_cols = (normed_cols * gain_two + columns_of(ln2_bias, member, own_width)).astype(half_type)

    hidden = scatter_sum(
        lambda owner: jnp.dot(
            two_cols, columns_of(w_fc1, owner, own_hidden), preferred_element_type=float_type
        )
    )
    hidden = hidden + columns_of(fc1_bias, member, own_hidden)

    def qkv_part(owner):
        return jnp.concatenate(
            [
                jnp.dot(
                    one_cols,
                    columns_of(w_qkv[:, i * D : (i + 1) * D], owner, own_width),
                    preferred_element_type=float_type,
                )
                for i in range(3)
            ],
            1,
        )

    d_act = contract_last(upstream, w_fc2)
    d_mixed_b = contract_last(upstream, w_out).astype(half_type)
    act_b = gelu_exact(hidden).astype(half_type)
    d_hidden = d_act * gelu_slope(hidden)
    d_hidden_b = d_hidden.astype(half_type)
    down_part = contract_first(act_b, upstream).astype(half_type)
    hidden_group = gather_along(d_hidden_b, 1)
    qkv = scatter_sum(qkv_part)
    up_part = contract_first(two_cols, hidden_group).astype(half_type)
    d_two = contract_last(hidden_group, w_fc1)

    split = (seq_total, own_heads, HEAD)
    q_bias = columns_of(qv_bias[0], member, own_width)
    v_bias = columns_of(qv_bias[1], member, own_width)
    query = (qkv[:, :own_width] + q_bias).reshape(split)
    keys = qkv[:, own_width : 2 * own_width].reshape(split)
    value_b = (qkv[:, 2 * own_width :] + v_bias).astype(half_type).reshape(split)
    query_b = rotate(query, cosine, sine).astype(half_type)
    keys_b = rotate(keys, cosine, sine).astype(half_type)
    d_mixed_h = d_mixed_b.reshape(split)
    allowed = all_pos[None, :, None] >= all_pos[None, None, :]
    raw = (
        jnp.einsum("qhd,khd->hqk", query_b, keys_b, preferred_element_type=float_type)
        * score_scale
    )
    scores = jnp.where(allowed, raw, NEGATIVE)
    highest = jnp.max(scores, -1, keepdims=True)
    log_total = highest + jnp.log(jnp.sum(jnp.exp(scores - highest), -1, keepdims=True))
    prob_f = jnp.exp(scores - log_total)
    prob_b = prob_f.astype(half_type)
    mixed = (
        jnp.einsum("hqk,khd->qhd", prob_b, value_b, preferred_element_type=float_type)
        .astype(half_type)
        .reshape(seq_total, own_width)
    )
    proj_part = contract_first(mixed, upstream)
    d_prob = jnp.einsum("qhd,khd->hqk", d_mixed_h, value_b, preferred_element_type=float_type)
    delta = jnp.sum(prob_f * d_prob, -1, keepdims=True)
    d_score = (prob_f * (d_prob - delta) * score_scale).astype(half_type)
    d_query = jnp.einsum("hqk,khd->qhd", d_score, keys_b, preferred_element_type=float_type)
    d_query = unrotate(d_query, cosine, sine).reshape(seq_total, own_width)
    d_keys = jnp.einsum("hqk,qhd->khd", d_score, query_b, preferred_element_type=float_type)
    d_keys = unrotate(d_keys, cosine, sine).reshape(seq_total, own_width)
    d_value = jnp.einsum("hqk,qhd->khd", prob_b, d_mixed_h, preferred_element_type=float_type)
    d_value = d_value.reshape(seq_total, own_width)

    d_own = jnp.concatenate([d_query, d_keys, d_value], 1).astype(half_type)
    qkv_group = jnp.zeros((seq_total, 3 * D), half_type)
    for step in range(group_size):
        block = d_own if step == 0 else shift(d_own, step)
        owner = (member - step) % group_size
        for i in range(3):
            qkv_group = lax.dynamic_update_slice_in_dim(
                qkv_group,
                block[:, i * own_width : (i + 1) * own_width],
                i * D + owner * own_width,
                1,
            )
    qkv_part_grad = contract_first(one_cols, qkv_group)
    d_one = contract_last(qkv_group, w_qkv)

    branch_whole = jnp.dot(mixed, w_out, preferred_element_type=float_type) + jnp.dot(
        act_b, w_fc2, preferred_element_type=float_type
    )
    branches = scatter_sum(lambda owner: rows_of(branch_whole, owner, tok_count))
    result = (tokens[0].astype(float_type) + branches + fc2_bias).astype(half_type)

    small = jnp.concatenate(
        [
            jnp.sum(d_one * normed_cols, 0),
            jnp.sum(d_one, 0),
            jnp.sum(d_two * normed_cols, 0),
            jnp.sum(d_two, 0),
            jnp.sum(d_query, 0),
            jnp.sum(d_value, 0),
            jnp.sum(columns_of(upstream, member, own_width).astype(float_type), 0),
            jnp.sum(d_hidden, 0),
        ]
    )
    used = small.shape[0]
    small = jnp.pad(small, (0, -used % (16 * D))).reshape(-1, D)
    proj_part = jnp.concatenate([proj_part, small]).astype(half_type)
    down_grad, up_grad, qkv_grad, proj_grad = rep_sum(
        [down_part, up_part, qkv_part_grad, proj_part]
    )
    small = proj_grad[own_width:].astype(float_type).reshape(-1)[:used]
    proj_grad = proj_grad[:own_width]
    pieces = [small[i * own_width : (i + 1) * own_width] for i in range(7)]

    scaled = d_one * gain_one + d_two * gain_two
    scaled_rows = jnp.zeros((tok_count, D), float_type)
    for step in range(group_size):
        block = rows_of(scaled, (member + step) % group_size, tok_count)
        if step > 0:
            block = shift(block, step)
        owner = (member - step) % group_size
        scaled_rows = lax.dynamic_update_slice_in_dim(scaled_rows, block, owner * own_width, 1)
    own_inputs = tokens[0].astype(float_type)
    own_centre = own_inputs - jnp.mean(own_inputs, -1, keepdims=True)
    own_rstd = lax.rsqrt(jnp.mean(own_centre * own_centre, -1, keepdims=True) + EPS)
    own_normed = own_centre * own_rstd
    grad_in = cotangent[0].astype(float_type) + own_rstd * (
        scaled_rows
        - jnp.mean(scaled_rows, -1, keepdims=True)
        - own_normed * jnp.mean(scaled_rows * own_normed, -1, keepdims=True)
    )
    return (
        result[None],
        grad_in[None],
        pieces[0],
        pieces[1],
        pieces[2],
        pieces[3],
        qkv_grad.astype(float_type),
        jnp.stack([pieces[4], pieces[5]]),
        proj_grad.astype(float_type),
        up_grad.astype(float_type),
        small[7 * own_width :],
        down_grad.astype(float_type),
        pieces[6],
    )


def solution(mesh):
    placed = (
        P("rep", "grp", None),
        P("rep", "grp", None),
        P("rep", None),
        P(),
        P(),
        P(),
        P(),
        P("grp", None),
        P(),
        P("grp", None),
        P("grp", None),
        P(),
        P("grp", None),
        P(),
    )
    return jax.shard_map(
        body,
        mesh=mesh,
        in_specs=placed,
        out_specs=(
            P("rep", "grp", None),
            P("rep", "grp", None),
            P("grp"),
            P("grp"),
            P("grp"),
            P("grp"),
            P("grp", None),
            P(None, "grp"),
            P("grp", None),
            P("grp", None),
            P("grp"),
            P("grp", None),
            P("grp"),
        ),
        check_vma=False,
    )
```

time: 944 us -> 409 us (0.43)
  waiting for transfers between devices: 656 us -> 281 us
  blocking collectives: 114 us -> 0 us
  matrix products: 88.5 us -> 45.8 us
  other arithmetic: 16 us -> 35.5 us
  local copies, waits for them, and re-layouts: 38 us -> 22.1 us
    all_gather x6 -> x0, waiting for transfers between devices: 273 us -> none  [the longest x1 98.9 us: body(): lax.all_gather(w_fc2, 'grp', axis=0, tiled=True)]
    psum x1, waiting for transfers between devices: 360 us -> 219 us  [rep_sum(): return lax.psum([value.astype(jnp.bfloat16) for value in values], 'rep')]
    psum x1 -> x0, blocking collectives: 63.4 us -> none  [body(): lax.psum((input_rows_grad, proj_rows_grad, down_rows_grad, gain_one, shif...]
    ppermute x0 -> x7, waiting for transfers between devices: none -> 62.2 us  [shift(): lax.ppermute(value, 'grp', [(i, (i + distance) % size) for i in range(siz...]
    all_gather x3 -> x0, blocking collectives: 43.5 us -> none  [the longest x1 20.2 us: body(): lax.all_gather(upstream, 'grp', axis=0, tiled=True)]
    convert_element_type x1 -> x5, other arithmetic: 1.89 us -> 17.7 us  [the longest x1 6.82 us: body(): up_grad.astype(float_type)]
    all_to_all x4 -> x0, waiting for transfers between devices: 15 us -> none  [the longest x1 10.1 us: body(): lax.all_to_all(act_b, 'grp', split_axis=1, concat_axis=0, tiled=True)]
    dot_general x9 -> x15, matrix products: 37.3 us -> 22.9 us  [the longest x2 5.99 us: body(): jnp.dot(two_cols, columns_of(w_fc1, owner, own_hidden), preferred_element...]
  transfers between devices with their start and end apart: 13 -> 8, of which waited for: 10 -> 6; matrix products, arithmetic and copies ran while one was open for 13% -> 15% of each run, Pallas kernels for 0% -> 0%
where the time goes in v1:
time: 409 us; the launch traced here: 408 us
  waiting for transfers between devices  281 us (69%)
  matrix products  45.8 us (11%)
  other arithmetic  35.5 us (9%)
  local copies, waits for them, and re-layouts  22.1 us (5%)
  between operations  14.9 us (4%)
  starting transfers between devices  9.22 us (2%)
    psum x1, waiting for transfers between devices, rep_sum(): return lax.psum([value.astype(jnp.bfloat16) for value in values], 'rep')  219 us
    ppermute x7, waiting for transfers between devices, shift(): lax.ppermute(value, 'grp', [(i, (i + distance) % size) for i in range(siz...  62.2 us
    dot_general x4, matrix products, contract_first(): lax.dot_general(left, right, (((0,), (0,)), ((), ())), preferred_element_...  11.2 us
    ppermute x7, starting transfers between devices, shift(): lax.ppermute(value, 'grp', [(i, (i + distance) % size) for i in range(siz...  9.18 us
  transfers between devices with their start and end apart: 8, of which 6 were waited for; matrix products, arithmetic and copies ran while one was open for 15% of the time, Pallas kernels for 0%

profile of v1, /device:TPU:0, one launch (start us, length us, event | category | flops | bytes accessed | tf_op | source)
XLA Modules:
  0.0 408.3 jit_solution(5606942444900132914)
XLA Ops:
  7.4 2.0 pad_maximum_fusion.3
  9.4 3.0 collective-permute-start
  13.1 2.2 fusion.85
  15.3 9.3 %collective-permute-done = bf16[128,2048]{1,0:T(8,128)(2,1)} collective-permute-done((bf16[128,2048]{1,0:T(8,128)(2,1)}, bf16[128,2048]{1,0:T(8,128)(2,1)}, u32[]{:S(2)}, u32[]{:S(2)}) %collective-permute-start) | collective-permute-done | bytes 524320 | tf_op jit(solution)/shard_map/ppermute | solution.py:76
  24.6 1.2 constant_dynamic-update-slice_fusion.6
  25.8 0.9 fusion.86
  27.4 1.8 convolution_convert_fusion.3
  29.1 1.7 collective-permute-start.2
  32.0 0.9 pad_maximum_fusion.1
  33.2 1.2 convolution_convert_fusion.5
  34.4 1.9 copy.53
  36.3 1.0 dynamic-slice_reduce_fusion
  37.3 1.3 fusion.50
  39.3 31.3 %collective-permute-done.1 = bf16[256,1536]{1,0:T(8,128)(2,1)} collective-permute-done((bf16[256,1536]{1,0:T(8,128)(2,1)}, bf16[256,1536]{1,0:T(8,128)(2,1)}, u32[]{:S(2)}, u32[]{:S(2)}) %collective-permute-start.1) | collective-permute-done | bytes 786464 | tf_op jit(solution)/shard_map/ppermute | solution.py:76
  70.6 1.3 maximum_add_fusion
  72.0 0.8 slice_add_fusion
  73.4 0.5 fusion.90
  74.3 1.8 copy.49
  76.1 2.8 fusion.92
  79.0 4.1 %fusion.23 = f32[256,8,64]{0,2,1:T(8,128)} fusion(f32[8,256,256]{1,2,0:T(8,128)} %fusion.92, f32[8,256,256]{1,2,0:T(8,128)S(1)} %get-tuple-element.69, f32[8,256]{1,0:T(8,128)S(1)} %log_add_fusion, bf16[256,8,48]{0,2,1:T(8,128)(2,1)} %copy-done.32, bf16[256,8,8]{0,2,1:T(8,128)(2,1)} %copy-done.37, bf16[256,8,8]{0,2,1:T(8,128)(2,1)S(1)} %copy-done.36), kind=kOutput, calls=%fused_computation.30 | convolution fusion | flops 71567616 | bytes 4988928 | tf_op jit(solution)/shard_map/hqk,qhd->khd/dot_general | solution.py:229
  83.1 4.1 fusion.20
  87.1 2.2 fusion.87
  89.4 0.7 slice.229
  90.3 0.7 fusion.56
  91.1 0.9 pad_maximum_fusion.7
  92.1 0.7 copy-done.23
  92.8 2.0 pad_maximum_fusion.2
  94.7 1.5 collective-permute-start.4
  96.4 1.1 constant_dynamic-update-slice_fusion.5
  97.6 0.5 convolution_convert_fusion.6
  98.1 0.7 copy-done.21
  99.6 4.2 %multiply_convert_fusion.1 = (bf16[256,2048]{1,0:T(8,128)(2,1)}, f32[256,2048]{1,0:T(8,128)S(1)}) fusion(f32[2048]{0:T(1024)S(1)} %dynamic-slice-done, bf16[256,2048]{1,0:T(8,128)(2,1)} %collective-permute-done.2, bf16[512,4096]{1,0:T(8,128)(2,1)} %param.24, s32[]{:T(128)} %select_n.150, f32[512]{0:T(512)S(1)} %dynamic_slice.75, f32[512]{0:T(512)S(1)} %dynamic_slice.74, ...), kind=kOutput, calls=%fused_computation.14 | convolution fusion | flops 541720576 | bytes 6830596 | tf_op jit(solution)/shard_map/dot_general | solution.py:169
  104.0 3.2 constant_dynamic-update-slice_fusion.2
  107.2 1.3 copy-done.4
  108.6 0.6 collective-permute-start.5
  109.1 1.7 reduce_sum.179
  110.8 4.6 %convolution_convert_fusion.2 = bf16[2048,1024]{1,0:T(8,128)(2,1)} fusion(bf16[256,2048]{1,0:T(8,128)(2,1)} %get-tuple-element.71, bf16[256,2048]{1,0:T(8,128)(2,1)S(1)} %copy-done.3), kind=kOutput, calls=%fused_computation.3 | convolution fusion | flops 1075838976 | bytes 5767168 | tf_op jit(solution)/shard_map/dot_general | solution.py:69
  115.5 1.0 slice_dynamic-update-slice_fusion.2
  116.5 1.0 slice_dynamic-update-slice_fusion.1
  117.5 1.0 slice_dynamic-update-slice_fusion
  118.4 2.7 convolution_convert_fusion.1
  121.2 1.0 fusion.93
  122.2 13.2 %collective-permute-done.5 = bf16[256,2048]{1,0:T(8,128)(2,1)} collective-permute-done((bf16[256,2048]{1,0:T(8,128)(2,1)}, bf16[256,2048]{1,0:T(8,128)(2,1)}, u32[]{:S(2)}, u32[]{:S(2)}) %collective-permute-start.5) | collective-permute-done | bytes 1048608 | tf_op jit(solution)/shard_map/ppermute | solution.py:76
  135.4 1.3 constant_dynamic-update-slice_fusion.1
  136.7 3.4 convolution_convert_fusion
  140.2 2.2 multiply_reduce_fusion.2
  144.2 1.1 pad_maximum_fusion
  145.3 0.9 copy-done.9
  146.6 3.5 fusion.91
  150.3 1.3 collective-permute-start.6
  151.5 0.5 convolution_add_fusion
  152.0 0.9 collective-permute-start.3
  152.9 6.0 %collective-permute-done.6 = f32[128,512]{1,0:T(8,128)S(1)} collective-permute-done((f32[128,512]{1,0:T(8,128)S(1)}, f32[128,512]{1,0:T(8,128)S(1)}, u32[]{:S(2)}, u32[]{:S(2)}) %collective-permute-start.6) | collective-permute-done | bytes 262176 | tf_op jit(solution)/shard_map/ppermute | solution.py:76
  159.2 2.5 collective-permute-done.3
  161.7 1.1 fusion.40
  162.8 218.5 %all-reduce.4.cloned.1.call-done = (bf16[528,1024]{1,0:T(8,128)(2,1)}, bf16[512,3072]{1,0:T(8,128)(2,1)}, bf16[512,4096]{1,0:T(8,128)(2,1)}, bf16[2048,1024]{1,0:T(8,128)(2,1)}) async-done(((bf16[528,1024]{1,0:T(8,128)(2,1)}, bf16[512,3072]{1,0:T(8,128)(2,1)}, bf16[512,4096]{1,0:T(8,128)(2,1)}, bf16[2048,1024]{1,0:T(8,128)(2,1)}), (bf16[528,1024]{1,0:T(8,128)(2,1)}, bf16[512,3072]{1,0:T(8,128)(2,1)}, ...) | async-done | bytes 12615696 | tf_op jit(solution)/shard_map/psum | solution.py:115
  381.3 0.8 convert_bitcast_fusion
  382.1 2.8 slice_convert_fusion
  384.9 0.6 fusion.88
  385.5 0.6 slice.186
  386.1 6.8 %convert_element_type.122 = f32[512,4096]{1,0:T(8,128)} convert(bf16[512,4096]{1,0:T(8,128)(2,1)} %get-tuple-element.21) | non-fusion elementwise | flops 2097152 | bytes 12582912 | tf_op jit(solution)/shard_map/convert_element_type | solution.py:304
  392.9 4.4 %convert_element_type.124 = f32[2048,1024]{1,0:T(8,128)} convert(bf16[2048,1024]{1,0:T(8,128)(2,1)S(1)} %copy-done.12) | non-fusion elementwise | flops 2097152 | bytes 12582912 | tf_op jit(solution)/shard_map/convert_element_type | solution.py:306
  397.3 3.5 convert_element_type.119
  400.8 0.6 pad_maximum_fusion.12
  (160 shorter events, 8.6 us)
Async XLA Ops:
  7.2 26.1 %copy-start = (bf16[512,1024]{1,0:T(8,128)(2,1)S(1)}, bf16[512,1024]{1,0:T(8,128)(2,1)}, u32[]{:S(2)}) copy-start(bf16[512,1024]{1,0:T(8,128)(2,1)} %param.23) | copy-start | bytes 3145732
  7.2 5.2 %copy-start.41 = (f32[1024]{0:T(1024)S(1)}, f32[1024]{0:T(1024)}, u32[]{:S(2)}) copy-start(f32[1024]{0:T(1024)} %param.19) | copy-start | bytes 12292
  7.2 5.3 %copy-start.42 = (f32[1024]{0:T(1024)S(1)}, f32[1024]{0:T(1024)}, u32[]{:S(2)}) copy-start(f32[1024]{0:T(1024)} %param.20) | copy-start | bytes 12292
  7.2 5.3 %copy-start.43 = (f32[1024]{0:T(1024)S(1)}, f32[1024]{0:T(1024)}, u32[]{:S(2)}) copy-start(f32[1024]{0:T(1024)} %param.17) | copy-start | bytes 12292
  7.2 5.4 %copy-start.44 = (f32[1024]{0:T(1024)S(1)}, f32[1024]{0:T(1024)}, u32[]{:S(2)}) copy-start(f32[1024]{0:T(1024)} %param.18) | copy-start | bytes 12292
  7.2 5.5 %copy-start.39 = (f32[2,1024]{1,0:T(2,128)S(1)}, f32[2,1024]{1,0:T(2,128)}, u32[]{:S(2)}) copy-start(f32[2,1024]{1,0:T(2,128)} %param.22) | copy-start | bytes 24580
  7.2 5.5 %copy-start.45 = (s32[1,4]{1,0:T(1,128)S(1)}, s32[1,4]{1,0:T(1,128)}, u32[]{:S(2)}) copy-start(s32[1,4]{1,0:T(1,128)} %param.16) | copy-start | bytes 52
  7.3 374.0 %all-reduce.4.cloned.1.call-start = ((), (), s32[]{:S(2)}) async-start(), calls=%async_computation | async-start | bytes 25231360 | tf_op jit(solution)/shard_map/psum | solution.py:115
  9.4 15.2 %collective-permute-start = (bf16[128,2048]{1,0:T(8,128)(2,1)}, bf16[128,2048]{1,0:T(8,128)(2,1)}, u32[]{:S(2)}, u32[]{:S(2)}) collective-permute-start(bf16[128,2048]{1,0:T(8,128)(2,1)} %get-tuple-element.48), channel_id=1, source_target_pairs={{0,1},{1,0},{2,3},{3,2},{4,5},{5,4},{6,7},{7,6},{8,9},{9,8},{10,11... | collective-permute-start | bytes 1572872 | tf_op jit(solution)/shard_map/ppermute | solution.py:76
  15.3 17.6 %copy-start.13 = (bf16[512,1024]{1,0:T(8,128)(2,1)}, bf16[512,1024]{1,0:T(8,128)(2,1)S(1)}, u32[]{:S(2)}) copy-start(bf16[512,1024]{1,0:T(8,128)(2,1)S(1)} %get-tuple-element.27) | copy-start | bytes 3145732
  15.3 17.6 %copy-start.15 = (bf16[512,1024]{1,0:T(8,128)(2,1)}, bf16[512,1024]{1,0:T(8,128)(2,1)S(1)}, u32[]{:S(2)}) copy-start(bf16[512,1024]{1,0:T(8,128)(2,1)S(1)} %get-tuple-element.28) | copy-start | bytes 3145732
  24.6 2.8 copy-start.25
  25.8 7.4 %copy-start.1 = (bf16[256,2048]{1,0:T(8,128)(2,1)}, bf16[256,2048]{1,0:T(8,128)(2,1)S(1)}, u32[]{:S(2)}) copy-start(bf16[256,2048]{1,0:T(8,128)(2,1)S(1)} %constant_dynamic-update-slice_fusion.6) | copy-start | bytes 3145732
  26.8 4.1 %copy-start.6 = (f32[256,1024]{1,0:T(8,128)}, f32[256,1024]{1,0:T(8,128)S(1)}, u32[]{:S(2)}) copy-start(f32[256,1024]{1,0:T(8,128)S(1)} %get-tuple-element.34) | copy-start | bytes 3145732
  29.1 70.1 %collective-permute-start.2 = (bf16[256,2048]{1,0:T(8,128)(2,1)}, bf16[256,2048]{1,0:T(8,128)(2,1)}, u32[]{:S(2)}, u32[]{:S(2)}) collective-permute-start(bf16[256,2048]{1,0:T(8,128)(2,1)} %convolution_convert_fusion.3), channel_id=1, source_target_pairs={{0,1},{1,0},{2,3},{3,2},{4,5},{5,4},{6,7},{7,6},{8,9},{9,8},{10,11... | collective-permute-start | bytes 3145736 | tf_op jit(solution)/shard_map/ppermute | solution.py:76
  33.0 37.7 %collective-permute-start.1 = (bf16[256,1536]{1,0:T(8,128)(2,1)}, bf16[256,1536]{1,0:T(8,128)(2,1)}, u32[]{:S(2)}, u32[]{:S(2)}) collective-permute-start(bf16[256,1536]{1,0:T(8,128)(2,1)} %pad_maximum_fusion.1), channel_id=1, source_target_pairs={{0,1},{1,0},{2,3},{3,2},{4,5},{5,4},{6,7},{7,6},{8,9},{9,8},{10,11... | collective-permute-start | bytes 2359304 | tf_op jit(solution)/shard_map/ppermute | solution.py:76
  34.4 4.2 %copy-start.14 = (bf16[512,1024]{1,0:T(8,128)(2,1)S(1)}, bf16[512,1024]{1,0:T(8,128)(2,1)}, u32[]{:S(2)}) copy-start(bf16[512,1024]{1,0:T(8,128)(2,1)} %copy-done.13) | copy-start | bytes 3145732
  73.2 0.7 copy-start.31
  73.3 0.7 copy-start.32
  73.3 0.7 copy-start.33
  73.4 0.6 copy-start.35
  73.4 0.6 copy-start.37
  74.3 4.6 %copy-start.36 = (bf16[256,8,8]{0,2,1:T(8,128)(2,1)S(1)}, bf16[256,8,8]{0,2,1:T(8,128)(2,1)}, u32[]{:S(2)}) copy-start(bf16[256,8,8]{0,2,1:T(8,128)(2,1)} %copy-done.35) | copy-start | bytes 98308
  79.0 4.1 %copy-start.34 = (bf16[256,8,8]{0,2,1:T(8,128)(2,1)S(1)}, bf16[256,8,8]{0,2,1:T(8,128)(2,1)}, u32[]{:S(2)}) copy-start(bf16[256,8,8]{0,2,1:T(8,128)(2,1)} %copy-done.33) | copy-start | bytes 98308
  87.1 2.2 copy-start.29
  87.1 2.2 copy-start.30
  92.1 0.7 copy-start.23
  94.7 20.8 %collective-permute-start.4 = (bf16[256,1536]{0,1:T(8,128)(2,1)}, bf16[256,1536]{0,1:T(8,128)(2,1)}, u32[]{:S(2)}, u32[]{:S(2)}) collective-permute-start(bf16[256,1536]{0,1:T(8,128)(2,1)} %pad_maximum_fusion.2), channel_id=1, source_target_pairs={{0,1},{1,0},{2,3},{3,2},{4,5},{5,4},{6,7},{7,6},{8,9},{9,8},{10,11... | collective-permute-start | bytes 2359304 | tf_op jit(solution)/shard_map/ppermute | solution.py:76
  96.3 1.2 copy-start.24
  96.3 1.3 copy-start.20
  96.3 1.3 copy-start.19
  96.4 2.4 copy-start.2
  97.6 1.7 copy-start.10
  97.6 2.0 copy-start.7
  97.6 1.9 dynamic-slice-start
  98.1 0.7 copy-start.21
  99.6 4.5 %copy-start.46 = (bf16[2048,1024]{1,0:T(8,128)(2,1)S(1)}, bf16[2048,1024]{1,0:T(8,128)(2,1)}, u32[]{:S(2)}) copy-start(bf16[2048,1024]{1,0:T(8,128)(2,1)} %param.26) | copy-start | bytes 12582916
  107.2 1.3 copy-start.4
  108.6 2.3 copy-start.3
  108.6 26.8 %collective-permute-start.5 = (bf16[256,2048]{1,0:T(8,128)(2,1)}, bf16[256,2048]{1,0:T(8,128)(2,1)}, u32[]{:S(2)}, u32[]{:S(2)}) collective-permute-start(bf16[256,2048]{1,0:T(8,128)(2,1)} %get-tuple-element.24), channel_id=1, source_target_pairs={{0,1},{1,0},{2,3},{3,2},{4,5},{5,4},{6,7},{7,6},{8,9},{9,8},{10,11... | collective-permute-start | bytes 3145736 | tf_op jit(solution)/shard_map/ppermute | solution.py:76
  110.8 4.7 %copy-start.11 = (bf16[256,3072]{0,1:T(8,128)(2,1)S(1)}, bf16[256,3072]{0,1:T(8,128)(2,1)}, u32[]{:S(2)}) copy-start(bf16[256,3072]{0,1:T(8,128)(2,1)} %copy-done.10) | copy-start | bytes 4718596
  118.4 2.7 copy-start.16
  121.2 14.2 %copy-start.5 = (bf16[256,4096]{1,0:T(8,128)(2,1)S(1)}, bf16[256,4096]{1,0:T(8,128)(2,1)}, u32[]{:S(2)}) copy-start(bf16[256,4096]{1,0:T(8,128)(2,1)} %copy-done.4) | copy-start | bytes 6291460
  122.2 14.5 %copy-start.8 = (f32[256,1024]{1,0:T(8,128)S(1)}, f32[256,1024]{1,0:T(8,128)}, u32[]{:S(2)}) copy-start(f32[256,1024]{1,0:T(8,128)} %copy-done.6) | copy-start | bytes 3145732
  136.7 3.4 copy-start.26
  140.2 2.2 copy-start.38
  145.3 0.9 copy-start.9
  145.3 1.3 copy-start.18
  146.6 3.6 copy-start.28
  146.6 4.9 %copy-start.22 = (bf16[8,64,256]{2,1,0:T(8,128)(2,1)S(1)}, bf16[8,64,256]{2,1,0:T(8,128)(2,1)}, u32[]{:S(2)}) copy-start(bf16[8,64,256]{2,1,0:T(8,128)(2,1)} %copy-done.21) | copy-start | bytes 786436
  150.2 11.5 %copy-start.27 = (bf16[1,128,1024]{2,1,0:T(8,128)(2,1)S(1)}, bf16[1,128,1024]{2,1,0:T(8,128)(2,1)}, u32[]{:S(2)}) copy-start(bf16[1,128,1024]{2,1,0:T(8,128)(2,1)} %param.15) | copy-start | bytes 786436
  150.2 11.5 %copy-start.40 = (f32[1024]{0:T(1024)S(1)}, f32[1024]{0:T(1024)}, u32[]{:S(2)}) copy-start(f32[1024]{0:T(1024)} %param.27) | copy-start | bytes 12292
  150.3 8.6 %collective-permute-start.6 = (f32[128,512]{1,0:T(8,128)S(1)}, f32[128,512]{1,0:T(8,128)S(1)}, u32[]{:S(2)}, u32[]{:S(2)}) collective-permute-start(f32[128,512]{1,0:T(8,128)S(1)} %get-tuple-element.46), channel_id=1, source_target_pairs={{0,1},{1,0},{2,3},{3,2},{4,5},{5,4},{6,7},{7,6},{8,9},{9,8},{10,11... | collective-permute-start | bytes 786440 | tf_op jit(solution)/shard_map/ppermute | solution.py:76
  152.0 9.7 %collective-permute-start.3 = (bf16[128,1024]{1,0:T(8,128)(2,1)S(1)}, bf16[128,1024]{1,0:T(8,128)(2,1)S(1)}, u32[]{:S(2)}, u32[]{:S(2)}) collective-permute-start(bf16[128,1024]{1,0:T(8,128)(2,1)S(1)} %dynamic-slice_convert_fusion), channel_id=1, source_target_pairs={{0,1},{1,0},{2,3},{3,2},{4,5},{5,4},{6,7},{7,6},{8,9},{9,8},{10,11... | collective-permute-start | bytes 786440 | tf_op jit(solution)/shard_map/ppermute | solution.py:76
  386.1 6.8 %copy-start.12 = (bf16[2048,1024]{1,0:T(8,128)(2,1)S(1)}, bf16[2048,1024]{1,0:T(8,128)(2,1)}, u32[]{:S(2)}) copy-start(bf16[2048,1024]{1,0:T(8,128)(2,1)} %get-tuple-element.22) | copy-start | bytes 12582916
  392.9 4.4 %copy-start.17 = (bf16[512,3072]{1,0:T(8,128)(2,1)S(1)}, bf16[512,3072]{1,0:T(8,128)(2,1)}, u32[]{:S(2)}) copy-start(bf16[512,3072]{1,0:T(8,128)(2,1)} %get-tuple-element.20) | copy-start | bytes 9437188
Sparse Core Ops, SparseCore 0:
  145.4 235.8 all-reduce.3

commit v2 on v1

--- a/solution.py
+++ b/solution.py
@@ -111,8 +111,8 @@
     return lax.dynamic_slice_in_dim(value, owner * width, width, 0)
 
 
-def rep_sum(values):
-    return lax.psum([value.astype(jnp.bfloat16) for value in values], "rep")
+def rep_sum(value):
+    return lax.psum(value.astype(jnp.bfloat16), "rep")
 
 
 def body(
@@ -190,10 +190,10 @@
     act_b = gelu_exact(hidden).astype(half_type)
     d_hidden = d_act * gelu_slope(hidden)
     d_hidden_b = d_hidden.astype(half_type)
-    down_part = contract_first(act_b, upstream).astype(half_type)
+    down_grad = rep_sum(contract_first(act_b, upstream))
     hidden_group = gather_along(d_hidden_b, 1)
     qkv = scatter_sum(qkv_part)
-    up_part = contract_first(two_cols, hidden_group).astype(half_type)
+    up_grad = rep_sum(contract_first(two_cols, hidden_group))
     d_two = contract_last(hidden_group, w_fc1)
 
     split = (seq_total, own_heads, HEAD)
@@ -220,7 +220,7 @@
         .astype(half_type)
         .reshape(seq_total, own_width)
     )
-    proj_part = contract_first(mixed, upstream)
+    proj_grad = rep_sum(contract_first(mixed, upstream))
     d_prob = jnp.einsum("qhd,khd->hqk", d_mixed_h, value_b, preferred_element_type=float_type)
     delta = jnp.sum(prob_f * d_prob, -1, keepdims=True)
     d_score = (prob_f * (d_prob - delta) * score_scale).astype(half_type)
@@ -243,7 +243,7 @@
                 i * D + owner * own_width,
                 1,
             )
-    qkv_part_grad = contract_first(one_cols, qkv_group)
+    qkv_grad = rep_sum(contract_first(one_cols, qkv_group))
     d_one = contract_last(qkv_group, w_qkv)
 
     branch_whole = jnp.dot(mixed, w_out, preferred_element_type=float_type) + jnp.dot(
@@ -264,14 +264,7 @@
             jnp.sum(d_hidden, 0),
         ]
     )
-    used = small.shape[0]
-    small = jnp.pad(small, (0, -used % (16 * D))).reshape(-1, D)
-    proj_part = jnp.concatenate([proj_part, small]).astype(half_type)
-    down_grad, up_grad, qkv_grad, proj_grad = rep_sum(
-        [down_part, up_part, qkv_part_grad, proj_part]
-    )
-    small = proj_grad[own_width:].astype(float_type).reshape(-1)[:used]
-    proj_grad = proj_grad[:own_width]
+    small = lax.psum(small, "rep")
     pieces = [small[i * own_width : (i + 1) * own_width] for i in range(7)]
 
     scaled = d_one * gain_one + d_two * gain_two

time: 409 us -> 371 us (0.907)
  waiting for transfers between devices: 281 us -> 189 us
  blocking collectives: 0 us -> 61.4 us
  local copies, waits for them, and re-layouts: 22.1 us -> 17.6 us
  other arithmetic: 35.5 us -> 31.4 us
    psum x1, waiting for transfers between devices: 219 us -> 140 us  [rep_sum(): return lax.psum(value.astype(jnp.bfloat16), 'rep')]
    psum x0 -> x1, blocking collectives: none -> 61.4 us  [body(): small = lax.psum(small, 'rep')]
    ppermute x7, waiting for transfers between devices: 62.2 us -> 48.4 us  [shift(): lax.ppermute(value, 'grp', [(i, (i + distance) % size) for i in range(siz...]
  transfers between devices with their start and end apart: 8 -> 8, of which waited for: 6 -> 6; matrix products, arithmetic and copies ran while one was open for 15% -> 18% of each run, Pallas kernels for 0% -> 0%
where the time goes in v2:
time: 371 us
  waiting for transfers between devices  189 us (51%)
  blocking collectives  61.4 us (17%)
  matrix products  47.1 us (13%)
  other arithmetic  31.4 us (8%)
  local copies, waits for them, and re-layouts  17.6 us (5%)
  between operations  15.1 us (4%)
  starting transfers between devices  9.45 us (3%)
    psum x1, waiting for transfers between devices, rep_sum(): return lax.psum(value.astype(jnp.bfloat16), 'rep')  140 us
    psum x1, blocking collectives, body(): small = lax.psum(small, 'rep')  61.4 us
    ppermute x7, waiting for transfers between devices, shift(): lax.ppermute(value, 'grp', [(i, (i + distance) % size) for i in range(siz...  48.4 us
    dot_general x4, matrix products, contract_first(): lax.dot_general(left, right, (((0,), (0,)), ((), ())), preferred_element_...  10.8 us
    dot_general x4, matrix products, contract_last(): lax.dot_general(left, right, (((1,), (1,)), ((), ())), preferred_element_...  9.47 us
    ppermute x7, starting transfers between devices, shift(): lax.ppermute(value, 'grp', [(i, (i + distance) % size) for i in range(siz...  9.41 us
  transfers between devices with their start and end apart: 8, of which 6 were waited for; matrix products, arithmetic and copies ran while one was open for 18% of the time, Pallas kernels for 0%

profile of v2, /device:TPU:0, one launch (start us, length us, event | category | flops | bytes accessed | tf_op | source)
XLA Modules:
  0.0 370.6 jit_solution(803730685587997409)
XLA Ops:
  7.4 2.0 pad_maximum_fusion.2
  9.4 3.0 collective-permute-start
  13.1 2.2 fusion.85
  15.3 9.3 %collective-permute-done = bf16[128,2048]{1,0:T(8,128)(2,1)} collective-permute-done((bf16[128,2048]{1,0:T(8,128)(2,1)}, bf16[128,2048]{1,0:T(8,128)(2,1)}, u32[]{:S(2)}, u32[]{:S(2)}) %collective-permute-start) | collective-permute-done | bytes 524320 | tf_op jit(solution)/shard_map/ppermute | solution.py:76
  24.6 1.1 constant_dynamic-update-slice_fusion.6
  25.8 1.0 fusion.86
  27.1 0.5 convolution_convert_fusion.5
  28.8 1.0 pad_maximum_fusion
  29.8 1.7 collective-permute-start.1
  31.5 1.8 convolution_convert_fusion.3
  33.3 0.8 copy.53
  34.1 0.5 collective-permute-start.2
  34.6 1.3 fusion.52
  36.0 1.3 fusion.50
  37.6 12.9 %collective-permute-done.1 = bf16[256,1536]{1,0:T(8,128)(2,1)} collective-permute-done((bf16[256,1536]{1,0:T(8,128)(2,1)}, bf16[256,1536]{1,0:T(8,128)(2,1)}, u32[]{:S(2)}, u32[]{:S(2)}) %collective-permute-start.1) | collective-permute-done | bytes 786464 | tf_op jit(solution)/shard_map/ppermute | solution.py:76
  50.5 1.3 maximum_add_fusion
  52.2 0.7 slice.210
  52.9 0.8 copy.49
  54.1 1.5 fusion.90
  56.0 1.8 fusion.87
  57.8 1.8 fusion.92
  59.6 4.1 %fusion.20 = f32[256,8,64]{0,2,1:T(8,128)} fusion(f32[8,256,256]{1,2,0:T(8,128)} %fusion.92, f32[8,256,256]{1,2,0:T(8,128)S(1)} %get-tuple-element.69, f32[8,256]{1,0:T(8,128)S(1)} %log_add_fusion, bf16[256,8,48]{0,2,1:T(8,128)(2,1)} %copy-done.27, bf16[256,8,8]{0,2,1:T(8,128)(2,1)S(1)} %copy-done.35, bf16[256,8,8]{0,2,1:T(8,128)(2,1)} %copy-done.36), kind=kOutput, calls=%fused_computation.29 | convolution fusion | flops 71567616 | bytes 4988928 | tf_op jit(solution)/shard_map/hqk,khd->qhd/dot_general | solution.py:227
  63.7 4.1 %fusion.23 = f32[256,8,64]{0,2,1:T(8,128)} fusion(f32[8,256,256]{1,2,0:T(8,128)} %fusion.92, f32[8,256,256]{1,2,0:T(8,128)S(1)} %get-tuple-element.69, f32[8,256]{1,0:T(8,128)S(1)} %log_add_fusion, bf16[256,8,48]{0,2,1:T(8,128)(2,1)} %slice.210, bf16[256,8,8]{0,2,1:T(8,128)(2,1)S(1)} %copy-done.33, bf16[256,8,8]{0,2,1:T(8,128)(2,1)S(1)} %get-tuple-element.40), kind=kOutput, calls=%fused_computation.30 | convolution fusion | flops 71567616 | bytes 4988928 | tf_op jit(solution)/shard_map/hqk,qhd->khd/dot_general | solution.py:229
  67.7 1.1 slice.208
  68.8 1.0 add_convert_fusion.2
  69.8 1.0 slice.154
  70.9 0.7 copy-done.12
  71.7 1.8 collective-permute-start.4
  74.3 0.8 copy-done.2
  75.0 1.4 convolution_convert_fusion.4
  76.5 2.5 multiply_convert_fusion.1
  79.3 3.2 constant_dynamic-update-slice_fusion.2
  82.8 3.3 convolution_convert_fusion.2
  86.1 6.1 %collective-permute-done.4 = bf16[256,1536]{0,1:T(8,128)(2,1)S(1)} collective-permute-done((bf16[256,1536]{0,1:T(8,128)(2,1)S(1)}, bf16[256,1536]{0,1:T(8,128)(2,1)S(1)}, u32[]{:S(2)}, u32[]{:S(2)}) %collective-permute-start.4) | collective-permute-done | bytes 786464 | tf_op jit(solution)/shard_map/ppermute | solution.py:76
  92.3 2.7 convolution_convert_fusion.1
  95.0 15.5 %collective-permute-done.5 = bf16[256,2048]{1,0:T(8,128)(2,1)S(1)} collective-permute-done((bf16[256,2048]{1,0:T(8,128)(2,1)S(1)}, bf16[256,2048]{1,0:T(8,128)(2,1)S(1)}, u32[]{:S(2)}, u32[]{:S(2)}) %collective-permute-start.5) | collective-permute-done | bytes 1048608 | tf_op jit(solution)/shard_map/ppermute | solution.py:76
  110.6 3.4 convolution_convert_fusion
  114.1 0.9 copy-done.6
  115.1 0.6 copy-done.44
  115.9 0.6 add_rsqrt_fusion.1
  116.5 1.6 convert_reduce_fusion.1
  118.1 0.7 reduce_sum.177
  118.7 1.1 fusion.55
  119.9 4.5 %fusion.91 = f32[256,1024]{1,0:T(8,128)S(1)} fusion(bf16[256,2048]{1,0:T(8,128)(2,1)} %copy-done.16, bf16[2048,1024]{1,0:T(8,128)(2,1)} %param.26), kind=kOutput, calls=%fused_computation.172 | convolution fusion | flops 1073741824 | bytes 6291456 | tf_op jit(solution)/shard_map/dot_general | solution.py:249
  124.5 0.5 convolution_add_fusion
  125.0 1.0 copy-done.13
  125.9 0.7 dynamic-slice_convert_fusion
  126.7 1.5 collective-permute-start.3
  128.1 1.8 reduce_sum.179
  130.0 3.6 fusion.93
  134.0 2.2 multiply_reduce_fusion.2
  136.4 61.4 %psum.35 = f32[5632]{0:T(1024)S(1)} all-reduce(f32[5632]{0:T(1024)S(1)} %constant_dynamic-update-slice_fusion.8), channel_id=1, replica_groups=mesh['rep'=16,'grp'=2] {'rep'}, use_global_device_ids=true, to_apply=%region_18.19 | all-reduce | flops 5632 | bytes 45056 | tf_op jit(solution)/shard_map/psum | solution.py:267
  197.8 0.6 slice.167
  198.4 1.1 constant_dynamic-slice_fusion
  199.5 0.6 collective-permute-start.6
  200.1 0.6 fusion.88
  200.7 0.6 pad_maximum_fusion.11
  201.3 4.7 %collective-permute-done.6 = f32[128,512]{1,0:T(8,128)S(1)} collective-permute-done((f32[128,512]{1,0:T(8,128)S(1)}, f32[128,512]{1,0:T(8,128)S(1)}, u32[]{:S(2)}, u32[]{:S(2)}) %collective-permute-start.6) | collective-permute-done | bytes 262176 | tf_op jit(solution)/shard_map/ppermute | solution.py:76
  206.3 2.0 fusion.40
  208.3 140.1 %all-reduce.3.cloned.1.call-done = (bf16[512,3072]{1,0:T(8,128)(2,1)}, bf16[512,1024]{1,0:T(8,128)(2,1)}, bf16[512,4096]{1,0:T(8,128)(2,1)}, bf16[2048,1024]{1,0:T(8,128)(2,1)}) async-done(((bf16[512,3072]{1,0:T(8,128)(2,1)}, bf16[512,1024]{1,0:T(8,128)(2,1)}, bf16[512,4096]{1,0:T(8,128)(2,1)}, bf16[2048,1024]{1,0:T(8,128)(2,1)}), (bf16[512,3072]{1,0:T(8,128)(2,1)}, bf16[512,1024]{1,0:T(8,128)(2,1)}, ...) | async-done | bytes 12582928 | tf_op jit(solution)/shard_map/psum | solution.py:115
  348.4 2.9 convert_element_type.120
  351.3 3.5 convert_element_type.118
  354.8 4.5 %convert_element_type.122 = f32[512,4096]{1,0:T(8,128)} convert(bf16[512,4096]{1,0:T(8,128)(2,1)S(1)} %copy-done.9) | non-fusion elementwise | flops 2097152 | bytes 12582912 | tf_op jit(solution)/shard_map/convert_element_type | solution.py:297
  359.3 4.4 %convert_element_type.124 = f32[2048,1024]{1,0:T(8,128)} convert(bf16[2048,1024]{1,0:T(8,128)(2,1)S(1)} %copy-done.8) | non-fusion elementwise | flops 2097152 | bytes 12582912 | tf_op jit(solution)/shard_map/convert_element_type | solution.py:299
  (170 shorter events, 6.6 us)
Async XLA Ops:
  7.2 19.9 %copy-start = (bf16[512,1024]{1,0:T(8,128)(2,1)S(1)}, bf16[512,1024]{1,0:T(8,128)(2,1)}, u32[]{:S(2)}) copy-start(bf16[512,1024]{1,0:T(8,128)(2,1)} %param.23) | copy-start | bytes 3145732
  7.2 5.2 %copy-start.52 = (s32[1,4]{1,0:T(1,128)S(1)}, s32[1,4]{1,0:T(1,128)}, u32[]{:S(2)}) copy-start(s32[1,4]{1,0:T(1,128)} %param.16) | copy-start | bytes 52
  7.2 5.3 %copy-start.48 = (f32[1024]{0:T(1024)S(1)}, f32[1024]{0:T(1024)}, u32[]{:S(2)}) copy-start(f32[1024]{0:T(1024)} %param.19) | copy-start | bytes 12292
  7.2 5.3 %copy-start.49 = (f32[1024]{0:T(1024)S(1)}, f32[1024]{0:T(1024)}, u32[]{:S(2)}) copy-start(f32[1024]{0:T(1024)} %param.20) | copy-start | bytes 12292
  7.2 5.4 %copy-start.50 = (f32[1024]{0:T(1024)S(1)}, f32[1024]{0:T(1024)}, u32[]{:S(2)}) copy-start(f32[1024]{0:T(1024)} %param.17) | copy-start | bytes 12292
  7.2 5.5 %copy-start.51 = (f32[1024]{0:T(1024)S(1)}, f32[1024]{0:T(1024)}, u32[]{:S(2)}) copy-start(f32[1024]{0:T(1024)} %param.18) | copy-start | bytes 12292
  7.2 5.5 %copy-start.43 = (f32[2,1024]{1,0:T(2,128)S(1)}, f32[2,1024]{1,0:T(2,128)}, u32[]{:S(2)}) copy-start(f32[2,1024]{1,0:T(2,128)} %param.22) | copy-start | bytes 24580
  7.3 341.1 %all-reduce.3.cloned.1.call-start = ((), (), s32[]{:S(2)}) async-start(), calls=%async_computation | async-start | bytes 25165824 | tf_op jit(solution)/shard_map/psum | solution.py:115
  9.4 15.2 %collective-permute-start = (bf16[128,2048]{1,0:T(8,128)(2,1)}, bf16[128,2048]{1,0:T(8,128)(2,1)}, u32[]{:S(2)}, u32[]{:S(2)}) collective-permute-start(bf16[128,2048]{1,0:T(8,128)(2,1)} %get-tuple-element.48), channel_id=1, source_target_pairs={{0,1},{1,0},{2,3},{3,2},{4,5},{5,4},{6,7},{7,6},{8,9},{9,8},{10,11... | collective-permute-start | bytes 1572872 | tf_op jit(solution)/shard_map/ppermute | solution.py:76
  12.7 14.9 %copy-start.39 = (f32[512]{0:T(512)}, f32[512]{0:T(512)S(1)}, u32[]{:S(2)}) copy-start(f32[512]{0:T(512)S(1)} %dynamic_slice.64) | copy-start | bytes 6148
  13.1 40.9 %copy-start.30 = (f32[256,8]{0,1:T(8,128)}, f32[256,8]{0,1:T(8,128)S(1)}, u32[]{:S(2)}) copy-start(f32[256,8]{0,1:T(8,128)S(1)} %get-tuple-element.65) | copy-start | bytes 24580
  13.1 40.9 %copy-start.31 = (f32[256,8]{0,1:T(8,128)}, f32[256,8]{0,1:T(8,128)S(1)}, u32[]{:S(2)}) copy-start(f32[256,8]{0,1:T(8,128)S(1)} %get-tuple-element.66) | copy-start | bytes 24580
  15.3 12.5 %copy-start.11 = (bf16[512,1024]{1,0:T(8,128)(2,1)}, bf16[512,1024]{1,0:T(8,128)(2,1)S(1)}, u32[]{:S(2)}) copy-start(bf16[512,1024]{1,0:T(8,128)(2,1)S(1)} %get-tuple-element.27) | copy-start | bytes 3145732
  15.3 12.8 %copy-start.10 = (bf16[512,1024]{1,0:T(8,128)(2,1)}, bf16[512,1024]{1,0:T(8,128)(2,1)S(1)}, u32[]{:S(2)}) copy-start(bf16[512,1024]{1,0:T(8,128)(2,1)S(1)} %get-tuple-element.28) | copy-start | bytes 3145732
  25.7 1.9 copy-start.1
  26.8 4.7 %copy-start.3 = (f32[256,1024]{1,0:T(8,128)}, f32[256,1024]{1,0:T(8,128)S(1)}, u32[]{:S(2)}) copy-start(f32[256,1024]{1,0:T(8,128)S(1)} %get-tuple-element.34) | copy-start | bytes 3145732
  27.8 3.7 %copy-start.23 = (bf16[512,4096]{1,0:T(8,128)(2,1)S(1)}, bf16[512,4096]{1,0:T(8,128)(2,1)}, u32[]{:S(2)}) copy-start(bf16[512,4096]{1,0:T(8,128)(2,1)} %param.24) | copy-start | bytes 12582916
  29.8 20.7 %collective-permute-start.1 = (bf16[256,1536]{1,0:T(8,128)(2,1)}, bf16[256,1536]{1,0:T(8,128)(2,1)}, u32[]{:S(2)}, u32[]{:S(2)}) collective-permute-start(bf16[256,1536]{1,0:T(8,128)(2,1)} %pad_maximum_fusion), channel_id=1, source_target_pairs={{0,1},{1,0},{2,3},{3,2},{4,5},{5,4},{6,7},{7,6},{8,9},{9,8},{10,11... | collective-permute-start | bytes 2359304 | tf_op jit(solution)/shard_map/ppermute | solution.py:76
  34.1 42.3 %collective-permute-start.2 = (bf16[256,2048]{1,0:T(8,128)(2,1)}, bf16[256,2048]{1,0:T(8,128)(2,1)}, u32[]{:S(2)}, u32[]{:S(2)}) collective-permute-start(bf16[256,2048]{1,0:T(8,128)(2,1)} %convolution_convert_fusion.3), channel_id=1, source_target_pairs={{0,1},{1,0},{2,3},{3,2},{4,5},{5,4},{6,7},{7,6},{8,9},{9,8},{10,11... | collective-permute-start | bytes 3145736 | tf_op jit(solution)/shard_map/ppermute | solution.py:76
  54.0 1.6 copy-start.27
  54.1 1.6 copy-start.32
  54.1 1.6 copy-start.34
  54.1 1.5 copy-start.36
  54.1 1.9 copy-start.19
  55.6 2.1 copy-start.17
  56.0 7.7 %copy-start.28 = (f32[8,256]{1,0:T(8,128)}, f32[8,256]{1,0:T(8,128)S(1)}, u32[]{:S(2)}) copy-start(f32[8,256]{1,0:T(8,128)S(1)} %log_add_fusion) | copy-start | bytes 24580
  56.0 3.6 copy-start.35
  59.6 4.1 %copy-start.33 = (bf16[256,8,8]{0,2,1:T(8,128)(2,1)S(1)}, bf16[256,8,8]{0,2,1:T(8,128)(2,1)}, u32[]{:S(2)}) copy-start(bf16[256,8,8]{0,2,1:T(8,128)(2,1)} %copy-done.32) | copy-start | bytes 98308
  67.7 3.9 %copy-start.20 = (bf16[256,8,64]{0,2,1:T(8,128)(2,1)S(1)}, bf16[256,8,64]{0,2,1:T(8,128)(2,1)}, u32[]{:S(2)}) copy-start(bf16[256,8,64]{0,2,1:T(8,128)(2,1)} %get-tuple-element.45) | copy-start | bytes 786436
  70.8 0.8 copy-start.12
  71.6 2.1 copy-start.18
  71.6 2.1 copy-start.29
  71.7 20.5 %collective-permute-start.4 = (bf16[256,1536]{0,1:T(8,128)(2,1)S(1)}, bf16[256,1536]{0,1:T(8,128)(2,1)S(1)}, u32[]{:S(2)}, u32[]{:S(2)}) collective-permute-start(bf16[256,1536]{0,1:T(8,128)(2,1)S(1)} %pad_maximum_fusion.1), channel_id=1, source_target_pairs={{0,1},{1,0},{2,3},{3,2},{4,5},{5,4},{6,7},{7,6},{8,9},{9,8},{10,11... | collective-permute-start | bytes 2359304 | tf_op jit(solution)/shard_map/ppermute | solution.py:76
  73.5 2.9 copy-start.24
  73.7 1.4 copy-start.2
  73.8 2.7 copy-start.4
  73.8 2.7 dynamic-slice-start
  74.3 2.2 copy-start.21
  76.5 2.7 copy-start.53
  79.0 3.8 %copy-start.16 = (bf16[256,2048]{1,0:T(8,128)(2,1)}, bf16[256,2048]{1,0:T(8,128)(2,1)S(1)}, u32[]{:S(2)}) copy-start(bf16[256,2048]{1,0:T(8,128)(2,1)S(1)} %get-tuple-element.71) | copy-start | bytes 3145732
  82.4 28.0 %collective-permute-start.5 = (bf16[256,2048]{1,0:T(8,128)(2,1)S(1)}, bf16[256,2048]{1,0:T(8,128)(2,1)S(1)}, u32[]{:S(2)}, u32[]{:S(2)}) collective-permute-start(bf16[256,2048]{1,0:T(8,128)(2,1)S(1)} %get-tuple-element.24), channel_id=1, source_target_pairs={{0,1},{1,0},{2,3},{3,2},{4,5},{5,4},{6,7},{7,6},{8,9},{9,8},{10,11... | collective-permute-start | bytes 3145736 | tf_op jit(solution)/shard_map/ppermute | solution.py:76
  92.3 2.7 copy-start.7
  114.0 0.9 copy-start.6
  114.0 4.0 %copy-start.38 = (f32[8,64]{1,0:T(8,128)S(1)}, f32[8,64]{1,0:T(8,128)}, u32[]{:S(2)}) copy-start(f32[8,64]{1,0:T(8,128)} %get-tuple-element.44) | copy-start | bytes 6148
  115.1 0.6 copy-start.44
  119.9 4.5 %copy-start.22 = (bf16[8,64,256]{2,1,0:T(8,128)(2,1)S(1)}, bf16[8,64,256]{2,1,0:T(8,128)(2,1)}, u32[]{:S(2)}) copy-start(bf16[8,64,256]{2,1,0:T(8,128)(2,1)} %copy-done.21) | copy-start | bytes 786436
  124.9 1.0 copy-start.13
  126.7 79.6 %collective-permute-start.3 = (bf16[128,1024]{1,0:T(8,128)(2,1)}, bf16[128,1024]{1,0:T(8,128)(2,1)}, u32[]{:S(2)}, u32[]{:S(2)}) collective-permute-start(bf16[128,1024]{1,0:T(8,128)(2,1)} %dynamic-slice_convert_fusion), channel_id=1, source_target_pairs={{0,1},{1,0},{2,3},{3,2},{4,5},{5,4},{6,7},{7,6},{8,9},{9,8},{10,11... | collective-permute-start | bytes 786440 | tf_op jit(solution)/shard_map/ppermute | solution.py:76
  129.9 3.7 copy-start.5
  129.9 4.1 %copy-start.25 = (bf16[512,4096]{1,0:T(8,128)(2,1)S(1)}, bf16[512,4096]{1,0:T(8,128)(2,1)}, u32[]{:S(2)}) copy-start(bf16[512,4096]{1,0:T(8,128)(2,1)} %param.24) | copy-start | bytes 12582916
  129.9 4.1 %copy-start.40 = (f32[512]{0:T(512)S(1)}, f32[512]{0:T(512)}, u32[]{:S(2)}) copy-start(f32[512]{0:T(512)} %copy-done.39) | copy-start | bytes 6148
  134.0 2.2 copy-start.37
  134.0 2.3 copy-start.42
  134.0 2.3 copy-start.41
  136.2 69.8 %copy-start.45 = (f32[128]{0:T(128)S(1)}, f32[128]{0:T(128)}, u32[]{:S(2)}) copy-start(f32[128]{0:T(128)} %copy-done.44) | copy-start | bytes 1540
  136.2 69.8 %copy-start.47 = (f32[128]{0:T(128)S(1)}, f32[128]{0:T(128)}, u32[]{:S(2)}) copy-start(f32[128]{0:T(128)} %add_rsqrt_fusion.1) | copy-start | bytes 1540
  136.2 70.0 %copy-start.14 = (f32[256,1024]{1,0:T(8,128)S(1)}, f32[256,1024]{1,0:T(8,128)}, u32[]{:S(2)}) copy-start(f32[256,1024]{1,0:T(8,128)} %copy-done.13) | copy-start | bytes 3145732
  136.2 70.0 %copy-start.26 = (bf16[1,128,1024]{2,1,0:T(8,128)(2,1)S(1)}, bf16[1,128,1024]{2,1,0:T(8,128)(2,1)}, u32[]{:S(2)}) copy-start(bf16[1,128,1024]{2,1,0:T(8,128)(2,1)} %param.15) | copy-start | bytes 786436
  136.2 70.1 %copy-start.46 = (f32[1024]{0:T(1024)S(1)}, f32[1024]{0:T(1024)}, u32[]{:S(2)}) copy-start(f32[1024]{0:T(1024)} %param.27) | copy-start | bytes 12292
  199.5 6.4 %collective-permute-start.6 = (f32[128,512]{1,0:T(8,128)S(1)}, f32[128,512]{1,0:T(8,128)S(1)}, u32[]{:S(2)}, u32[]{:S(2)}) collective-permute-start(f32[128,512]{1,0:T(8,128)S(1)} %get-tuple-element.46), channel_id=1, source_target_pairs={{0,1},{1,0},{2,3},{3,2},{4,5},{5,4},{6,7},{7,6},{8,9},{9,8},{10,11... | collective-permute-start | bytes 786440 | tf_op jit(solution)/shard_map/ppermute | solution.py:76
  348.4 2.9 copy-start.15
  351.3 3.5 copy-start.9
  354.8 4.5 %copy-start.8 = (bf16[2048,1024]{1,0:T(8,128)(2,1)S(1)}, bf16[2048,1024]{1,0:T(8,128)(2,1)}, u32[]{:S(2)}) copy-start(bf16[2048,1024]{1,0:T(8,128)(2,1)} %get-tuple-element.22) | copy-start | bytes 12582916
Sparse Core Ops, SparseCore 0:
  114.2 234.1 all-reduce.2
